TPU v7x, 32 devices: a whole 2x2x4 slice. The times are simulated.
32 devices in a mesh: dp: 8 (over z, y), tensor: 4 (over x, core).
Axes of the slice: x: 2, y: 2, z: 4, core: 2. Of those that a mesh axis runs over, the one named last changes fastest.
Arguments:
- tokens: bfloat16 [8192, 768], P('dp'), may hold values from -6 to 6
- cotangent: bfloat16 [8192, 768], P('dp'), may hold values from -6 to 6
- gain_attn: float32 [768], replicated, may hold values from 0.5 to 1.5
- prefix_len: int32 [8], P('dp'), may hold values from 102 to 512
- bucket_ids: int32 [2047], replicated, may hold values from 0 to 31
- pos_bias: float32 [32, 12], P(None, 'tensor'), may hold values from -4 to 4
- w_qkv: bfloat16 [3, 768, 768], P(None, None, 'tensor'), may hold values from -0.21875 to 0.21875
- w_attn_out: bfloat16 [768, 768], P('tensor'), may hold values from -2.5 to 2.5
- gain_ffn: float32 [768], replicated, may hold values from 0.5 to 1.5
- w_router: bfloat16 [768, 4], replicated, may hold values from -0.4375 to 0.4375
- expert_ids: int32 [8192, 2], P('dp'), may hold values from 0 to 3, all different within a row; in each aligned block of 1024 rows (0 to 1023, 1024 to 2047, ...) at most 640 rows name the same one
- w_expert_in: bfloat16 [4, 768, 3072], P(None, None, 'tensor'), may hold values from -0.21875 to 0.21875
- w_expert_out: bfloat16 [4, 3072, 768], P(None, 'tensor'), may hold values from -0.21875 to 0.21875
Outputs:
- out: bfloat16 [8192, 768], P('dp', 'tensor')
- grad_tokens: float32 [8192, 768], P('dp', 'tensor')
- grad_gain_attn: float32 [768], P('dp')
- grad_pos_bias: float32 [32, 12], P(None, 'tensor')
- grad_w_qkv: float32 [3, 768, 768], P(None, 'dp', 'tensor')
- grad_w_attn_out: float32 [768, 768], P('tensor', 'dp')
- grad_gain_ffn: float32 [768], P('dp')
- grad_w_router: float32 [768, 4], P('dp')
- grad_w_expert_in: float32 [4, 768, 3072], P(None, 'dp', 'tensor')
- grad_w_expert_out: float32 [4, 3072, 768], P(None, 'tensor', 'dp')
Inputs may be any that keep to these rules, and one draw needn't show every extreme that they name: `expert_ids`: each row names two different experts; in the rows of one sequence no expert is named by more than 640 rows.
All inputs are finite; a program needn't handle non-finite values.
Results may differ from a plain program's by a relative error of at most 0.014.
Values sent between devices are 32-bit elements; how exact they have to be, the bound alone decides.
No kernel may reach another device: no remote copies, remote signals or barrier semaphores. Data moves between devices by JAX's collectives and lax.ppermute only.
A program may use at most 192 MiB of HBM per device.

v0:
```python
import jax
import jax.numpy as jnp
from jax import lax
from jax.sharding import PartitionSpec as P

CAP = 640


EPS = 1e-06
HIGH = lax.Precision.HIGHEST


def norm_rows(values, gain_vec):
    factor = lax.rsqrt(jnp.mean(values * values, axis=1, keepdims=True) + EPS)
    return (values * factor * gain_vec, factor)


def norm_back(values, factor, gain_vec, upstream):
    weighted = upstream * gain_vec
    inner_sum = jnp.mean(weighted * values, axis=1, keepdims=True)
    d_values = factor * weighted - values * (factor * factor * factor) * inner_sum
    d_gain = jnp.sum(upstream * values * factor, axis=0)
    return (d_values, d_gain)


def slot_positions(routes, experts, capacity):
    flat_ids = routes.reshape(-1)
    marks = (flat_ids[:, None] == jnp.arange(experts, dtype=jnp.int32)[None, :]).astype(jnp.int32)
    before = jnp.cumsum(marks, axis=0, dtype=jnp.int32) - marks
    within = jnp.sum(before * marks, axis=1, dtype=jnp.int32)
    return flat_ids * capacity + within


def band_bias(table_slice, block_rows, length):
    width = block_rows + length - 1
    head_part = table_slice[:, length - 1 :: -1]
    tail_part = table_slice[:, width - 1 : length - 1 : -1]
    spacer = jnp.zeros((table_slice.shape[0], 1), table_slice.dtype)
    period = jnp.concatenate([head_part, spacer, tail_part], axis=1)
    tiled = jnp.tile(period, (1, block_rows))[:, : block_rows * width]
    return tiled.reshape(table_slice.shape[0], block_rows, width)[:, :, :length]


def score_block(row_start, block_rows, queries, key_heads, band, prefix):
    length = key_heads.shape[1]
    row_ids = row_start + jnp.arange(block_rows, dtype=jnp.int32)
    col_ids = jnp.arange(length, dtype=jnp.int32)
    query_rows = lax.dynamic_slice_in_dim(queries, row_start, block_rows, 1)
    scores = (
        jnp.einsum("hqd,hkd->hqk", query_rows, key_heads, preferred_element_type=jnp.float32)
        * 0.125
        + band
    )
    visible = (col_ids[None, :] <= row_ids[:, None]) | (col_ids[None, :] < prefix)
    return (jnp.where(visible[None], scores, -1e30), query_rows)


def on_device(
    tokens,
    cotangent,
    gain_attn,
    prefix_len,
    bucket_ids,
    pos_bias,
    w_qkv,
    w_attn_out,
    gain_ffn,
    w_router,
    expert_ids,
    w_expert_in,
    w_expert_out,
):
    length, model_width = tokens.shape
    head_count = pos_bias.shape[1]
    head_size = w_attn_out.shape[0] // head_count
    experts = w_router.shape[1]
    capacity = CAP
    block_rows = min(512, length)
    band_width = block_rows + length - 1
    starts = jnp.arange(length // block_rows, dtype=jnp.int32) * block_rows
    prefix = prefix_len[0]
    tokens_f = tokens.astype(jnp.float32)
    normed1, factor1 = norm_rows(tokens_f, gain_attn)
    normed1_b = normed1.astype(jnp.bfloat16)
    qkv_b = jnp.einsum("ld,cdf->clf", normed1_b, w_qkv, preferred_element_type=jnp.float32).astype(
        jnp.bfloat16
    )
    qkv_heads = qkv_b.reshape(3, length, head_count, head_size).transpose(0, 2, 1, 3)
    queries, key_heads, value_heads = (qkv_heads[0], qkv_heads[1], qkv_heads[2])
    bucket_marks = (
        bucket_ids[:, None] == jnp.arange(pos_bias.shape[0], dtype=jnp.int32)[None, :]
    ).astype(jnp.float32)
    bias_table = jnp.dot(pos_bias.T, bucket_marks.T, precision=HIGH)

    def make_band(table_slice):
        return band_bias(table_slice, block_rows, length)

    def forward_block(row_start):
        band = make_band(lax.dynamic_slice_in_dim(bias_table, row_start, band_width, 1))
        scores, query_rows = score_block(row_start, block_rows, queries, key_heads, band, prefix)
        row_peak = jnp.max(scores, axis=-1, keepdims=True)
        raised = jnp.exp(scores - row_peak)
        total_w = jnp.sum(raised, axis=-1, keepdims=True)
        softmax_b = (raised / total_w).astype(jnp.bfloat16)
        attended = jnp.einsum(
            "hqk,hkd->hqd", softmax_b, value_heads, preferred_element_type=jnp.float32
        )
        return (attended, (row_peak + jnp.log(total_w))[..., 0])

    attended_blocks, lse_blocks = lax.map(forward_block, starts)
    attended = (
        attended_blocks.transpose(1, 0, 2, 3)
        .reshape(head_count, length, head_size)
        .astype(jnp.bfloat16)
    )
    log_total = lse_blocks.transpose(1, 0, 2).reshape(head_count, length)
    attended_flat = attended.transpose(1, 0, 2).reshape(length, head_count * head_size)
    attn_part = jnp.dot(attended_flat, w_attn_out, preferred_element_type=jnp.float32)
    attn_branch = lax.psum(attn_part, "tensor")
    hidden = tokens_f + attn_branch
    normed2, factor2 = norm_rows(hidden, gain_ffn)
    normed2_b = normed2.astype(jnp.bfloat16)
    logits = jnp.dot(normed2_b, w_router, preferred_element_type=jnp.float32)
    softmax_r = jax.nn.softmax(logits, axis=-1)
    chosen = (expert_ids[:, :, None] == jnp.arange(experts, dtype=jnp.int32)[None, None, :]).astype(
        jnp.float32
    )
    gate_vals = jnp.sum(softmax_r[:, None, :] * chosen, axis=-1)
    slot_index = slot_positions(expert_ids, experts, capacity)
    token_index = jnp.repeat(jnp.arange(length, dtype=jnp.int32), 2)
    dispatched = (
        jnp.zeros((experts * capacity, model_width), jnp.bfloat16)
        .at[slot_index]
        .set(normed2_b[token_index])
    )
    dispatched = dispatched.reshape(experts, capacity, model_width)
    pre_act = jnp.einsum(
        "ecd,edf->ecf", dispatched, w_expert_in, preferred_element_type=jnp.float32
    )
    activated, gelu_pull = jax.vjp(jax.nn.gelu, pre_act)
    activated_b = activated.astype(jnp.bfloat16)
    expert_rows = jnp.einsum(
        "ecf,efd->ecd", activated_b, w_expert_out, preferred_element_type=jnp.float32
    )
    expert_rows = expert_rows.reshape(experts * capacity, model_width)
    picked = expert_rows[slot_index].reshape(length, 2, model_width)
    moe_part = jnp.sum(gate_vals[:, :, None] * picked, axis=1)
    moe_slice = lax.psum_scatter(moe_part, "tensor", scatter_dimension=1, tiled=True)
    slice_cols = moe_slice.shape[1]
    first_col = lax.axis_index("tensor") * slice_cols
    hidden_slice = lax.dynamic_slice_in_dim(hidden, first_col, slice_cols, 1)
    output = (hidden_slice + moe_slice).astype(jnp.bfloat16)
    upstream = cotangent.astype(jnp.float32)
    d_picked = (gate_vals[:, :, None] * upstream[:, None, :]).reshape(2 * length, model_width)
    d_rows = jnp.zeros((experts * capacity, model_width), jnp.float32).at[slot_index].set(d_picked)
    d_rows = d_rows.astype(jnp.bfloat16).reshape(experts, capacity, model_width)
    d_gates_part = jnp.sum(upstream[:, None, :] * picked, axis=-1)
    grad_w_out = jnp.einsum("ecf,ecd->efd", activated_b, d_rows, preferred_element_type=jnp.float32)
    d_activated = jnp.einsum(
        "ecd,efd->ecf", d_rows, w_expert_out, preferred_element_type=jnp.float32
    )
    d_pre = gelu_pull(d_activated)[0].astype(jnp.bfloat16)
    grad_w_in = jnp.einsum("ecd,ecf->edf", dispatched, d_pre, preferred_element_type=jnp.float32)
    d_dispatched = jnp.einsum(
        "ecf,edf->ecd", d_pre, w_expert_in, preferred_element_type=jnp.float32
    )
    d_dispatched = d_dispatched.reshape(experts * capacity, model_width)
    grad_w_in, grad_w_out = (
        lax.psum_scatter(grad_w_in, "dp", scatter_dimension=1, tiled=True),
        lax.psum_scatter(grad_w_out, "dp", scatter_dimension=2, tiled=True),
    )
    d_normed2_part = jnp.sum(d_dispatched[slot_index].reshape(length, 2, model_width), axis=1)
    d_normed2, d_gates = lax.psum((d_normed2_part, d_gates_part), "tensor")
    d_softmax_r = jnp.sum(d_gates[:, :, None] * chosen, axis=1)
    d_logits = softmax_r * (d_softmax_r - jnp.sum(softmax_r * d_softmax_r, axis=-1, keepdims=True))
    d_normed2 = d_normed2 + jnp.dot(d_logits, w_router.astype(jnp.float32).T, precision=HIGH)
    grad_router = jnp.dot(normed2_b.astype(jnp.float32).T, d_logits, precision=HIGH)
    d_hidden_norm, grad_gain_ffn = norm_back(hidden, factor2, gain_ffn, d_normed2)
    d_hidden = upstream + d_hidden_norm
    d_branch_b = d_hidden.astype(jnp.bfloat16)
    grad_w_o = jnp.einsum(
        "lf,ld->fd", attended_flat, d_branch_b, preferred_element_type=jnp.float32
    )
    d_attended = jnp.einsum(
        "ld,fd->lf", d_branch_b, w_attn_out, preferred_element_type=jnp.float32
    ).astype(jnp.bfloat16)
    d_heads = d_attended.reshape(length, head_count, head_size).transpose(1, 0, 2)

    def backward_block(carried, row_start):
        d_keys, d_values, d_table = carried
        table_slice = lax.dynamic_slice_in_dim(bias_table, row_start, band_width, 1)
        band, band_pull = jax.vjp(make_band, table_slice)
        scores, query_rows = score_block(row_start, block_rows, queries, key_heads, band, prefix)
        lse_rows = lax.dynamic_slice_in_dim(log_total, row_start, block_rows, 1)
        softmax_p = jnp.exp(scores - lse_rows[..., None])
        grad_rows = lax.dynamic_slice_in_dim(d_heads, row_start, block_rows, 1)
        d_softmax = jnp.einsum(
            "hqd,hkd->hqk", grad_rows, value_heads, preferred_element_type=jnp.float32
        )
        inner_sum = jnp.sum(softmax_p * d_softmax, axis=-1, keepdims=True)
        d_scores = (softmax_p * (d_softmax - inner_sum)).astype(jnp.bfloat16)
        d_query = (
            jnp.einsum("hqk,hkd->hqd", d_scores, key_heads, preferred_element_type=jnp.float32)
            * 0.125
        )
        d_keys = (
            d_keys
            + jnp.einsum("hqk,hqd->hkd", d_scores, query_rows, preferred_element_type=jnp.float32)
            * 0.125
        )
        d_values = d_values + jnp.einsum(
            "hqk,hqd->hkd",
            softmax_p.astype(jnp.bfloat16),
            grad_rows,
            preferred_element_type=jnp.float32,
        )
        d_slice = band_pull(d_scores.astype(jnp.float32))[0]
        old_slice = lax.dynamic_slice_in_dim(d_table, row_start, band_width, 1)
        d_table = lax.dynamic_update_slice_in_dim(d_table, old_slice + d_slice, row_start, 1)
        return ((d_keys, d_values, d_table), d_query)

    start_state = (
        jnp.zeros((head_count, length, head_size), jnp.float32),
        jnp.zeros((head_count, length, head_size), jnp.float32),
        jnp.zeros(bias_table.shape, jnp.float32),
    )
    (d_keys, d_values, d_table), d_query_blocks = lax.scan(backward_block, start_state, starts)
    d_queries = d_query_blocks.transpose(1, 0, 2, 3).reshape(head_count, length, head_size)
    d_qkv = jnp.stack([d_queries, d_keys, d_values]).transpose(0, 2, 1, 3)
    d_qkv = d_qkv.reshape(3, length, head_count * head_size).astype(jnp.bfloat16)
    grad_qkv = jnp.einsum("ld,clf->cdf", normed1_b, d_qkv, preferred_element_type=jnp.float32)
    d_normed1_part = jnp.einsum("clf,cdf->ld", d_qkv, w_qkv, preferred_element_type=jnp.float32)
    d_normed1 = lax.psum(d_normed1_part, "tensor")
    d_tokens_norm, grad_gain_attn = norm_back(tokens_f, factor1, gain_attn, d_normed1)
    d_tokens = lax.dynamic_slice_in_dim(d_hidden + d_tokens_norm, first_col, slice_cols, 1)
    grad_bias = jnp.dot(bucket_marks.T, d_table.T, precision=HIGH)
    grad_bias = lax.psum(grad_bias, "dp")
    grad_qkv, grad_w_o, grad_router, grad_gain_attn, grad_gain_ffn = (
        lax.psum_scatter(grad_qkv, "dp", scatter_dimension=1, tiled=True),
        lax.psum_scatter(grad_w_o, "dp", scatter_dimension=1, tiled=True),
        lax.psum_scatter(grad_router, "dp", scatter_dimension=0, tiled=True),
        lax.psum_scatter(grad_gain_attn, "dp", scatter_dimension=0, tiled=True),
        lax.psum_scatter(grad_gain_ffn, "dp", scatter_dimension=0, tiled=True),
    )
    return (
        output,
        d_tokens,
        grad_gain_attn,
        grad_bias,
        grad_qkv,
        grad_w_o,
        grad_gain_ffn,
        grad_router,
        grad_w_in,
        grad_w_out,
    )


def solution(mesh):
    in_specs = (
        P("dp", None),
        P("dp", None),
        P(),
        P("dp"),
        P(),
        P(None, "tensor"),
        P(None, None, "tensor"),
        P("tensor", None),
        P(),
        P(),
        P("dp", None),
        P(None, None, "tensor"),
        P(None, "tensor", None),
    )
    out_specs = (
        P("dp", "tensor"),
        P("dp", "tensor"),
        P("dp"),
        P(None, "tensor"),
        P(None, "dp", "tensor"),
        P("tensor", "dp"),
        P("dp"),
        P("dp", None),
        P(None, "dp", "tensor"),
        P(None, "tensor", "dp"),
    )
    return jax.shard_map(
        on_device, mesh=mesh, in_specs=in_specs, out_specs=out_specs, check_vma=False
    )
```

profile of v0, /device:TPU:0, one launch (start us, length us, event | category | flops | bytes accessed | tf_op | source)
XLA Modules:
  0.0 1227.1 jit_solution(6435000136080081666)
XLA Ops:
  13.8 142.5 %while.29 = (s32[]{:T(128)}, bf16[2,3,512,64]{2,3,1,0:T(8,128)(2,1)S(1)}, f32[2,3,512]{2,1,0:T(4,128)}, s32[2]{0:T(128)S(1)}, s32[]{:T(128)}, /*index=5*/bf16[3,...) while((s32[]{:T(128)}, ...), condition=%wide.region_4.5_spmd, body=%wide.region_1.4_spmd.sunk | while | flops 417857536 | bytes 112691408 | solution.py:110
  22.0 19.9 %copy.106 = f32[1,3,512,1536]{3,1,2,0:T(4,128)S(1)} copy(f32[1,3,512,1536]{3,2,1,0:T(8,128)S(1)} %broadcast_bitcast_fusion.4) | data formatting | bytes 18874368 | tf_op jit(solution)/shard_map/while
  60.8 15.6 %reshape.423 = f32[3,512,1535]{2,1,0:T(8,128)} reshape(f32[2357760]{0:T(1024)} %reshape.422) | data formatting | bytes 18862080 | tf_op jit(solution)/shard_map/while/body/eval_jaxpr/reshape | solution.py:41
  93.0 19.9 %copy.106 = f32[1,3,512,1536]{3,1,2,0:T(4,128)S(1)} copy(f32[1,3,512,1536]{3,2,1,0:T(8,128)S(1)} %broadcast_bitcast_fusion.4) | data formatting | bytes 18874368 | tf_op jit(solution)/shard_map/while
  131.8 15.6 %reshape.423 = f32[3,512,1535]{2,1,0:T(8,128)} reshape(f32[2357760]{0:T(1024)} %reshape.422) | data formatting | bytes 18862080 | tf_op jit(solution)/shard_map/while/body/eval_jaxpr/reshape | solution.py:41
  181.2 49.7 %all-reduce.11.cloned.1.call-done = f32[1024,768]{1,0:T(8,128)} async-done(((f32[1024,768]{1,0:T(8,128)}), f32[1024,768]{1,0:T(8,128)}) %all-reduce.11.cloned.1.call-update) | async-done | bytes 3145744 | tf_op jit(solution)/shard_map/psum | solution.py:119
  238.6 14.5 %scatter_custom_fusion.1 = f32[2560,768]{1,0:T(8,128)} fusion(s32[2048]{0:T(1024)S(1)} %bitcast.219, f32[2048,768]{1,0:T(8,128)} %mul.324, f32[]{:T(128)} %constant.56.clone.1, f32[2048]{0:T(1024)S(1)} %mul.321), kind=kCustom, calls=%fused_computation.68 | custom fusion | flops 1572864 | bytes 14163972 | tf_op jit(solution)/shard_map/scatter | solution.py:155
  258.6 27.8 %scatter_custom_fusion = bf16[2560,768]{1,0:T(8,128)(2,1)} fusion(s32[2048]{0:T(1024)S(1)} %bitcast.220, bf16[1024,768]{1,0:T(8,128)(2,1)} %copy-done.13, s32[2048]{0:T(1024)S(1)} %broadcast_clamp_fusion.1, bf16[]{:T(256)} %constant.31.clone.1), kind=kCustom, calls=%fused_computation.83 | custom fusion | bytes 3932672 | tf_op jit(solution)/shard_map/scatter | solution.py:134
  314.1 13.9 %gather_fusion.1 = f32[2048,768]{1,0:T(8,128)} fusion(f32[2560,768]{1,0:T(8,128)} %bitcast.196, s32[2048]{0:T(1024)S(1)} %broadcast_clamp_fusion), kind=kCustom, calls=%fused_computation.2 | custom fusion | bytes 12591104 | tf_op jit(solution)/shard_map/gather | solution.py:172
  359.8 14.2 %gather_fusion = f32[2048,768]{1,0:T(8,128)} fusion(f32[2560,768]{1,0:T(8,128)} %bitcast.195, s32[2048]{0:T(1024)S(1)} %broadcast_clamp_fusion), kind=kCustom, calls=%fused_computation.1 | custom fusion | bytes 12591104 | tf_op jit(solution)/shard_map/gather | solution.py:146
  382.2 17.1 %multiply_reduce_fusion.1 = (f32[1024,2]{1,0:T(8,128)S(1)}, f32[1024,768]{1,0:T(8,128)}) fusion(f32[1024,2,768]{2,1,0:T(2,128)} %reshape.333, f32[1024,768]{1,0:T(8,128)} %convert_element_type.85, f32[1024,2]{1,0:T(8,128)S(1)} %copy.71), kind=kLoop, calls=%fused_computation.67 | loop fusion | flops 5502976 | bytes 12599296 | tf_op jit(solution)/shard_map/reduce_sum | solution.py:157
  399.3 25.5 %psum.37 = f32[1024,2]{1,0:T(8,128)S(1)} all-reduce(f32[1024,2]{1,0:T(8,128)S(1)} %get-tuple-element.228), channel_id=1, replica_groups=mesh['dp'=8,'tensor'=4] {'tensor'}, use_global_device_ids=true, to_apply=%region_20.21 | all-reduce | flops 2048 | bytes 16384 | tf_op jit(solution)/shard_map/psum | solution.py:173
  446.4 254.4 %while.30 = (s32[]{:T(128)}, f32[3,1024,64]{1,2,0:T(8,128)}, f32[3,1024,64]{1,2,0:T(8,128)}, f32[3,2047]{1,0:T(4,128)}, bf16[2,3,512,64]{2,3,1,0:T(8,128)(2,1)},...) while((s32[]{:T(128)}, f32[3,1024,64]{1,2,0:T(8,128)}, ...), condition=%wide.region_27.28_spmd.clone, body=%wide.region_24.27_spmd.clone.sunk | while | flops 1029214720 | bytes 236708400 | solution.py:227
  480.8 19.9 %copy.108 = f32[1,3,512,1536]{3,1,2,0:T(4,128)S(1)} copy(f32[1,3,512,1536]{3,2,1,0:T(8,128)S(1)} %broadcast_bitcast_fusion.5) | data formatting | bytes 18874368 | tf_op jit(solution)/shard_map/while
  506.4 13.2 %reshape.425 = f32[2357760]{0:T(1024)} reshape(f32[3,785920]{1,0:T(4,128)} %slice.89) | data formatting | bytes 18862080 | tf_op jit(solution)/shard_map/while
  519.6 15.8 %reshape.426 = f32[3,512,1535]{2,1,0:T(8,128)} reshape(f32[2357760]{0:T(1024)} %reshape.425) | data formatting | bytes 18862080 | tf_op jit(solution)/shard_map/while/body/eval_jaxpr/jvp()/reshape | solution.py:41
  593.8 19.9 %copy.108 = f32[1,3,512,1536]{3,1,2,0:T(4,128)S(1)} copy(f32[1,3,512,1536]{3,2,1,0:T(8,128)S(1)} %broadcast_bitcast_fusion.5) | data formatting | bytes 18874368 | tf_op jit(solution)/shard_map/while
  632.6 15.8 %reshape.426 = f32[3,512,1535]{2,1,0:T(8,128)} reshape(f32[2357760]{0:T(1024)} %reshape.425) | data formatting | bytes 18862080 | tf_op jit(solution)/shard_map/while/body/eval_jaxpr/jvp()/reshape | solution.py:41
  756.1 22.1 %all-reduce.15.cloned.1.call-done = f32[1024,768]{1,0:T(8,128)} async-done(((f32[1024,768]{1,0:T(8,128)}), f32[1024,768]{1,0:T(8,128)}) %all-reduce.15.cloned.1.call-update) | async-done | bytes 3145744 | tf_op jit(solution)/shard_map/psum | solution.py:233
  783.0 37.3 %all-reduce.6 = (f32[768]{0:T(1024)S(1)}, f32[32,3]{0,1:T(4,128)}, f32[768]{0:T(1024)S(1)}) all-reduce(f32[768]{0:T(1024)S(1)} %get-tuple-element.230, f32[32,3]{0,1:T(4,128)S(1)} %fusion.56, f32[768]{0:T(1024)S(1)} %copy-done.37), channel_id=3, replica_groups=mesh['dp'=8,'tensor'=4] {'dp'}, use_global_device_ids=true, to_apply=%region_31.32.clone | all-reduce | flops 1632 | bytes 13056
  821.5 27.7 %reduce-scatter.21.cloned.1.call-done = f32[96,576]{1,0:T(8,128)} async-done(((f32[768,576]{1,0:T(8,128)}), f32[96,576]{1,0:T(8,128)}) %reduce-scatter.21.cloned.1.call-update) | async-done | bytes 221200
  851.1 37.5 %reduce-scatter.19.cloned.1.call-done = f32[192,1024]{1,0:T(8,128)} async-done(((f32[768,1024]{1,0:T(8,128)}), f32[192,1024]{1,0:T(8,128)}) %reduce-scatter.19.cloned.1.call-update) | async-done | bytes 786448
  896.6 158.3 %reduce-scatter.15.cloned.1.call-done = f32[4,96,768]{2,1,0:T(8,128)} async-done(((f32[4,768,768]{2,1,0:T(8,128)}), f32[4,96,768]{2,1,0:T(8,128)}) %reduce-scatter.15.cloned.1.call-update) | async-done | bytes 1179664 | tf_op jit(solution)/shard_map/reduce_scatter | solution.py:169
  1054.8 165.4 %reduce-scatter.17.cloned.1.call-done = f32[4,768,96]{1,2,0:T(8,128)} async-done(((f32[4,768,768]{1,2,0:T(8,128)}), f32[4,768,96]{1,2,0:T(8,128)}) %reduce-scatter.17.cloned.1.call-update) | async-done | bytes 1179664 | tf_op jit(solution)/shard_map/reduce_scatter | solution.py:170
  (346 shorter events, 403.1 us)
Async XLA Ops:
  7.2 223.8 %all-reduce.11.cloned.1.call-start = ((), (), s32[]{:S(2)}) async-start(), calls=%async_computation.6 | async-start | bytes 6291456 | tf_op jit(solution)/shard_map/psum | solution.py:119
  159.6 270.9 %all-reduce.13.cloned.1.call-start = ((), (), s32[]{:S(2)}) async-start(), calls=%async_computation.7 | async-start | bytes 6291456 | tf_op jit(solution)/shard_map/psum | solution.py:173
  181.2 54.3 %copy-start.29 = (f32[768]{0:T(1024)S(1)}, f32[768]{0:T(1024)}, u32[]{:S(2)}) copy-start(f32[768]{0:T(1024)} %param.25) | copy-start | bytes 9220
  234.4 18.7 %copy-start.26 = (f32[1024]{0:T(1024)}, f32[1024]{0:T(1024)S(1)}, u32[]{:S(2)}) copy-start(f32[1024]{0:T(1024)S(1)} %get-tuple-element.292) | copy-start | bytes 12292
  237.5 15.6 %copy-start.28 = (f32[1024]{0:T(1024)}, f32[1024]{0:T(1024)S(1)}, u32[]{:S(2)}) copy-start(f32[1024]{0:T(1024)S(1)} %get-tuple-element.293) | copy-start | bytes 12292
  237.5 15.6 %copy-start.33 = (f32[1024]{0:T(1024)}, f32[1024]{0:T(1024)S(1)}, u32[]{:S(2)}) copy-start(f32[1024]{0:T(1024)S(1)} %fusion.69) | copy-start | bytes 12292
  286.4 22.2 %slice-start.2 = ((s8[4718592]{0:T(1024)(128)(4,1)}), s8[4194304]{0:T(1024)(128)(4,1)S(1)}, s32[]{:S(2)}) async-start(s8[4718592]{0:T(1024)(128)(4,1)} %bitcast.224), calls=%async_computation.17 | async-start | bytes 8388608
  348.5 403.9 %reduce-scatter.25.cloned.1.call-start = ((), (), s32[]{:S(2)}) async-start(), calls=%async_computation.14 | async-start | bytes 442368
  430.5 323.9 %reduce-scatter.23.cloned.1.call-start = ((), (), s32[]{:S(2)}) async-start(), calls=%async_computation.13 | async-start | bytes 884736
  444.9 333.3 %all-reduce.15.cloned.1.call-start = ((), (), s32[]{:S(2)}) async-start(), calls=%async_computation.8 | async-start | bytes 6291456 | tf_op jit(solution)/shard_map/psum | solution.py:233
  467.9 12.8 %copy-start.1 = (bf16[3,1024,64]{1,2,0:T(8,128)(2,1)}, bf16[3,1024,64]{1,2,0:T(8,128)(2,1)S(1)}, u32[]{:S(2)}) copy-start(bf16[3,1024,64]{1,2,0:T(8,128)(2,1)S(1)} %get-tuple-element.535) | copy-start | bytes 1179652 | tf_op jit(solution)/shard_map/while
  467.9 12.8 %copy-start.8 = (bf16[3,1024,64]{1,2,0:T(8,128)(2,1)}, bf16[3,1024,64]{1,2,0:T(8,128)(2,1)S(1)}, u32[]{:S(2)}) copy-start(bf16[3,1024,64]{1,2,0:T(8,128)(2,1)S(1)} %get-tuple-element.534) | copy-start | bytes 1179652 | tf_op jit(solution)/shard_map/while
  467.9 12.8 %copy-start.11 = (bf16[3,1024,64]{1,2,0:T(8,128)(2,1)}, bf16[3,1024,64]{1,2,0:T(8,128)(2,1)S(1)}, u32[]{:S(2)}) copy-start(bf16[3,1024,64]{1,2,0:T(8,128)(2,1)S(1)} %get-tuple-element.538) | copy-start | bytes 1179652 | tf_op jit(solution)/shard_map/while
  467.9 12.8 %copy-start.14 = (bf16[3,1024,64]{1,2,0:T(8,128)(2,1)}, bf16[3,1024,64]{1,2,0:T(8,128)(2,1)S(1)}, u32[]{:S(2)}) copy-start(bf16[3,1024,64]{1,2,0:T(8,128)(2,1)S(1)} %get-tuple-element.539) | copy-start | bytes 1179652 | tf_op jit(solution)/shard_map/while
  519.6 23.6 %slice-start = ((s8[6291456]{0:T(1024)(128)(4,1)}), s8[2097152]{0:T(1024)(128)(4,1)S(1)}, s32[]{:S(2)}) async-start(s8[6291456]{0:T(1024)(128)(4,1)} %bitcast.190), calls=%async_computation.15 | async-start | bytes 4194304 | tf_op jit(solution)/shard_map/while
  581.0 12.8 %copy-start.8 = (bf16[3,1024,64]{1,2,0:T(8,128)(2,1)}, bf16[3,1024,64]{1,2,0:T(8,128)(2,1)S(1)}, u32[]{:S(2)}) copy-start(bf16[3,1024,64]{1,2,0:T(8,128)(2,1)S(1)} %get-tuple-element.534) | copy-start | bytes 1179652 | tf_op jit(solution)/shard_map/while
  581.0 12.8 %copy-start.11 = (bf16[3,1024,64]{1,2,0:T(8,128)(2,1)}, bf16[3,1024,64]{1,2,0:T(8,128)(2,1)S(1)}, u32[]{:S(2)}) copy-start(bf16[3,1024,64]{1,2,0:T(8,128)(2,1)S(1)} %get-tuple-element.538) | copy-start | bytes 1179652 | tf_op jit(solution)/shard_map/while
  632.6 23.5 %slice-start = ((s8[6291456]{0:T(1024)(128)(4,1)}), s8[2097152]{0:T(1024)(128)(4,1)S(1)}, s32[]{:S(2)}) async-start(s8[6291456]{0:T(1024)(128)(4,1)} %bitcast.190), calls=%async_computation.15 | async-start | bytes 4194304 | tf_op jit(solution)/shard_map/while
  709.1 140.0 %reduce-scatter.21.cloned.1.call-start = ((), (), s32[]{:S(2)}) async-start(), calls=%async_computation.12 | async-start | bytes 2211840
  721.9 166.7 %reduce-scatter.19.cloned.1.call-start = ((), (), s32[]{:S(2)}) async-start(), calls=%async_computation.11 | async-start | bytes 3932160
  725.5 329.3 %reduce-scatter.15.cloned.1.call-start = ((), (), s32[]{:S(2)}) async-start(), calls=%async_computation.9 | async-start | bytes 10616832 | tf_op jit(solution)/shard_map/reduce_scatter | solution.py:169
  736.5 483.8 %reduce-scatter.17.cloned.1.call-start = ((), (), s32[]{:S(2)}) async-start(), calls=%async_computation.10 | async-start | bytes 10616832 | tf_op jit(solution)/shard_map/reduce_scatter | solution.py:170
  756.1 26.9 %copy-start.37 = (f32[768]{0:T(1024)S(1)}, f32[768]{0:T(1024)}, u32[]{:S(2)}) copy-start(f32[768]{0:T(1024)} %get-tuple-element.226) | copy-start | bytes 9220
  756.1 133.9 %copy-start.35 = (f32[1024]{0:T(1024)S(1)}, f32[1024]{0:T(1024)}, u32[]{:S(2)}) copy-start(f32[1024]{0:T(1024)} %get-tuple-element.289) | copy-start | bytes 12292
  (51 other events, 209.4 us)
Sparse Core Ops, SparseCore 0:
  159.8 71.1 all-reduce.10
  348.6 76.9 all-reduce.12
  430.6 62.5 reduce-scatter.24
  496.3 62.3 reduce-scatter.22
  709.3 68.8 all-reduce.14
  781.5 67.6 reduce-scatter.20
  851.7 36.7 reduce-scatter.18
  892.7 162.0 reduce-scatter.14
  1059.0 161.2 reduce-scatter.16
where the time goes:
time: 1230 us
  waiting for transfers between devices  461 us (37%)
  local copies, waits for them, and re-layouts  400 us (33%)
  matrix products  138 us (11%)
  other arithmetic  107 us (9%)
  blocking collectives  62.8 us (5%)
  loops' own time  42.1 us (3%)
  between operations  15.4 us (1%)
    reduce_scatter x1, waiting for transfers between devices, on_device(): lax.psum_scatter(grad_w_out, 'dp', scatter_dimension=2, tiled=True)  165 us
    while x90, local copies, waits for them, and re-layouts  162 us
    reduce_scatter x1, waiting for transfers between devices, on_device(): lax.psum_scatter(grad_w_in, 'dp', scatter_dimension=1, tiled=True)  158 us
    reshape x6, local copies, waits for them, and re-layouts, band_bias(): return tiled.reshape(table_slice.shape[0], block_rows, width)[:, :, :length]  78 us
    unnamed x13, waiting for transfers between devices  65.3 us
    psum x1, waiting for transfers between devices, on_device(): attn_branch = lax.psum(attn_part, 'tensor')  49.7 us
    unnamed x1, blocking collectives  37.3 us
    another operation x1, loops' own time, on_device(): lax.scan(backward_block, start_state, starts)  35.2 us
  transfers between devices with their start and end apart: 9, of which 6 were waited for; matrix products, arithmetic and copies ran while one was open for 31% of the time, Pallas kernels for 0%

commit v1 on v0

v1 whole, which is shorter than its diff:
```python
import jax
import jax.numpy as jnp
from jax import lax
from jax.experimental import pallas as pl
from jax.experimental.pallas import tpu as pltpu
from jax.sharding import PartitionSpec as P

EPS = 1e-06
f32, bf16 = jnp.float32, jnp.bfloat16
NN = (((1,), (0,)), ((), ()))
NT = (((1,), (1,)), ((), ()))
TN = (((0,), (0,)), ((), ()))
VM = pl.BlockSpec(memory_space=pltpu.VMEM)
SM = pl.BlockSpec(memory_space=pltpu.SMEM)

CORE = [(0, 1), (1, 0), (2, 3), (3, 2)]
ACROSS = [(0, 2), (2, 0), (1, 3), (3, 1)]


def dot(a, b, dims=NN):
    return lax.dot_general(a, b, dims, preferred_element_type=f32)


def params(mib):
    return pltpu.CompilerParams(vmem_limit_bytes=mib << 20)


def cost(flops, moved):
    return pl.CostEstimate(flops=flops, transcendentals=0, bytes_accessed=moved)


def bucket_hits(ids_ref, buckets):
    ids = ids_ref[...]
    return ids == lax.broadcasted_iota(jnp.int32, (buckets, ids.shape[1]), 0)


def build_band(ids_ref, pb_ref, band):
    width = ids_ref.shape[1]
    hit = bucket_hits(ids_ref, pb_ref.shape[0])
    for h in range(band.shape[0]):
        rev = jnp.sum(jnp.where(hit, pb_ref[:, h : h + 1], 0.0), axis=0, keepdims=True)
        full = jnp.broadcast_to(rev, (128, width))
        band[h, :, :] = pltpu.roll(full, width - 127, 1, stride=1, stride_axis=0)[:, : width - 128]


def attn_fwd_kernel(
    prefix_ref, x_ref, gain_ref, w_ref, ids_ref, pb_ref,
    a_ref, q_ref, kt_ref, v_ref, os_ref, o_ref, band,
):
    heads, length, size = q_ref.shape
    flat = heads * size
    rows_at_once = 256
    build_band(ids_ref, pb_ref, band)

    def project(i, carry):
        rows = pl.ds(pl.multiple_of(i * rows_at_once, rows_at_once), rows_at_once)
        x = x_ref[rows, :].astype(f32)
        r = lax.rsqrt(jnp.mean(x * x, axis=1, keepdims=True) + EPS)
        a = (x * r * gain_ref[...]).astype(bf16)
        a_ref[rows, :] = a
        q = dot(a, w_ref[0]).astype(bf16) * 0.125
        k = dot(a, w_ref[1]).astype(bf16)
        v = dot(a, w_ref[2]).astype(bf16)
        for h in range(heads):
            part = slice(h * size, (h + 1) * size)
            q_ref[h, rows, :] = q[:, part]
            v_ref[h, rows, :] = v[:, part]
            kt_ref[h, :, rows] = k[:, part].T
        return carry

    lax.fori_loop(0, length // rows_at_once, project, 0)
    prefix = prefix_ref[0]
    half = length // 2

    def head(h, carry):
        for b in range(length // rows_at_once):
            nk = max(half, rows_at_once * (b + 1))
            s = dot(q_ref[h, b * rows_at_once : (b + 1) * rows_at_once, :], kt_ref[h, :, 0:nk])
            for sub in range(rows_at_once // 128):
                row0 = b * rows_at_once + sub * 128
                off = length - 128 - row0
                t = s[sub * 128 : (sub + 1) * 128, :] + band[h, :, off : off + nk]
                row = row0 + lax.broadcasted_iota(jnp.int32, (128, 1), 0)
                col = lax.broadcasted_iota(jnp.int32, (128, nk), 1)
                t = jnp.where(col < jnp.maximum(row + 1, prefix), t, -1e30)
                m = jnp.max(t, axis=1, keepdims=True)
                e = jnp.exp(t - m)
                total = jnp.sum(e, axis=1, keepdims=True)
                p = (e * (1.0 / total)).astype(bf16)
                os_ref[h, row0 : row0 + 128, 0:size] = dot(p, v_ref[h, 0:nk, :])
                os_ref[h, row0 : row0 + 128, size : 2 * size] = jnp.broadcast_to(
                    m + jnp.log(total), (128, size)
                )
        return carry

    lax.fori_loop(0, heads, head, 0)
    for h in range(heads):
        o = os_ref[h, :, 0:size].astype(bf16).astype(f32)
        o_ref[:, h * size : (h + 1) * size] = o[:half]
        o_ref[:, flat + h * size : flat + (h + 1) * size] = o[half:]


def attn_fwd(prefix, tokens, gain, w, ids, pb):
    length, width = tokens.shape
    heads = pb.shape[1]
    flat = w.shape[2]
    size = flat // heads
    sds = jax.ShapeDtypeStruct
    return pl.pallas_call(
        attn_fwd_kernel,
        out_shape=(
            sds((length, width), bf16),
            sds((heads, length, size), bf16),
            sds((heads, size, length), bf16),
            sds((heads, length, size), bf16),
            sds((heads, length, 2 * size), f32),
            sds((length // 2, 2 * flat), f32),
        ),
        in_specs=[SM] + [VM] * 5,
        out_specs=[VM] * 6,
        scratch_shapes=[pltpu.VMEM((heads, 128, 2 * length - 128), f32)],
        compiler_params=params(36),
        cost_estimate=cost(12_000_000_000, 8_000_000),
        name="attn_fwd",
    )(prefix, tokens, gain.reshape(1, width), w, ids, pb)


def attn_bwd_kernel(
    prefix_ref, t_ref, d0_ref, d1_ref, d2_ref, d3_ref, wo_ref, q_ref, kt_ref, v_ref, os_ref,
    ids_ref, pb_ref,
    g_ref, dpb_ref, band, dband, do_s, dot_s, qt_s, vt_s, dk_s, dv_s,
):
    heads, length, size = q_ref.shape
    rows_at_once = 256
    width = 2 * length
    half = length // 2
    build_band(ids_ref, pb_ref, band)
    dband[...] = jnp.zeros_like(dband)
    dk_s[...] = jnp.zeros_like(dk_s)
    dv_s[...] = jnp.zeros_like(dv_s)
    count = d0_ref.shape[0]
    for r, d_ref in enumerate((d0_ref, d1_ref, d2_ref, d3_ref)):
        rows = pl.ds(pl.multiple_of((t_ref[0] ^ r) * count, count), count)
        d = d_ref[...].astype(bf16)
        do = dot(d, wo_ref[...], NT).astype(bf16)
        dt = dot(wo_ref[...], d, NT).astype(bf16)
        for h in range(heads):
            do_s[h, rows, :] = do[:, h * size : (h + 1) * size]
            dot_s[h, :, rows] = dt[h * size : (h + 1) * size, :]

    def turn(i, carry):
        rows = pl.ds(pl.multiple_of(i * rows_at_once, rows_at_once), rows_at_once)
        for h in range(heads):
            qt_s[h, :, rows] = q_ref[h, rows, :].T
            vt_s[h, :, rows] = v_ref[h, rows, :].T
        return carry

    lax.fori_loop(0, length // rows_at_once, turn, 0)
    prefix = prefix_ref[0]

    def head(h, carry):
        for b in range(length // rows_at_once):
            nk = max(half, rows_at_once * (b + 1))
            blk = slice(b * rows_at_once, (b + 1) * rows_at_once)
            s = dot(q_ref[h, blk, :], kt_ref[h, :, 0:nk])
            dp = dot(do_s[h, blk, :], vt_s[h, :, 0:nk])
            ps, dss = [], []
            for sub in range(rows_at_once // 128):
                row0 = b * rows_at_once + sub * 128
                off = length - 128 - row0
                part = slice(sub * 128, (sub + 1) * 128)
                t = s[part, :] + band[h, :, off : off + nk]
                row = row0 + lax.broadcasted_iota(jnp.int32, (128, 1), 0)
                col = lax.broadcasted_iota(jnp.int32, (128, nk), 1)
                kept = os_ref[h, row0 : row0 + 128, :]
                t = jnp.where(col < jnp.maximum(row + 1, prefix), t, -1e30)
                p = jnp.exp(t - kept[:, size : size + 1])
                delta = jnp.sum(
                    do_s[h, row0 : row0 + 128, :].astype(f32) * kept[:, :size],
                    axis=1, keepdims=True,
                )
                ds = (p * (dp[part, :] - delta)).astype(bf16)
                dband[h, :, off : off + nk] += ds.astype(f32)
                ps.append(p.astype(bf16))
                dss.append(ds)
            p = jnp.concatenate(ps, 0)
            ds = jnp.concatenate(dss, 0)
            dk_s[h, :, 0:nk] += dot(qt_s[h, :, blk], ds)
            dv_s[h, :, 0:nk] += dot(dot_s[h, :, blk], p)
            g_ref[0, h, :, blk] = (dot(kt_ref[h, :, 0:nk], ds, NT) * 0.125).astype(bf16)
        g_ref[1, h] = dk_s[h].astype(bf16)
        g_ref[2, h] = dv_s[h].astype(bf16)
        return carry

    lax.fori_loop(0, heads, head, 0)
    hit = bucket_hits(ids_ref, dpb_ref.shape[0])
    cols = []
    for h in range(heads):
        d = jnp.concatenate([dband[h], jnp.zeros((128, 128), f32)], axis=1)
        n = 64
        while n >= 8:
            d = pltpu.roll(d[:n], n, 1) + d[n : 2 * n]
            n //= 2
        total = d[7:8]
        for r in range(7):
            total = total + pltpu.roll(d[r : r + 1], 7 - r, 1)
        cols.append(jnp.sum(jnp.where(hit, total, 0.0), axis=1, keepdims=True))
    dpb_ref[...] = jnp.concatenate(cols, axis=1)


def attn_bwd(prefix, t, shards, wo, q, kt, v, os, ids, pb):
    heads, length, size = q.shape
    sds = jax.ShapeDtypeStruct
    return pl.pallas_call(
        attn_bwd_kernel,
        out_shape=(sds((3, heads, size, length), bf16), sds(pb.shape, f32)),
        in_specs=[SM, SM] + [VM] * 11,
        out_specs=[VM] * 2,
        scratch_shapes=[pltpu.VMEM((heads, 128, 2 * length - 128), f32)] * 2
        + [pltpu.VMEM((heads, length, size), bf16)]
        + [pltpu.VMEM((heads, size, length), bf16)] * 3
        + [pltpu.VMEM((heads, size, length), f32)] * 2,
        compiler_params=params(40),
        cost_estimate=cost(12_000_000_000, 8_000_000),
        name="attn_bwd",
    )(prefix, t, *shards, wo, q, kt, v, os, ids, pb)


def proj_kernel(
    x_ref, o0, o1, o2, o3, w0, w1, w2, w3, gain_ref, router_ref, ids_ref,
    h_ref, b_ref, gates_ref, probs_ref,
):
    length = x_ref.shape[0]
    flat = w0.shape[0]
    experts = router_ref.shape[1]
    half = length // 2
    step = 256
    for i in range(length // step):
        rows = slice(i * step, (i + 1) * step)
        top = (i * step) % half
        lane = flat * ((i * step) // half)
        acc = x_ref[rows, :].astype(f32)
        for o, w in ((o0, w0), (o1, w1), (o2, w2), (o3, w3)):
            acc = acc + dot(o[top : top + step, lane : lane + flat].astype(bf16), w[...].astype(bf16))
        h_ref[rows, :] = acc
        r = lax.rsqrt(jnp.mean(acc * acc, axis=1, keepdims=True) + EPS)
        b = (acc * r * gain_ref[...]).astype(bf16)
        b_ref[rows, :] = b
        logits = dot(b, router_ref[...])
        e = jnp.exp(logits - jnp.max(logits, axis=1, keepdims=True))
        probs = e / jnp.sum(e, axis=1, keepdims=True)
        ids = ids_ref[rows, :]
        lanes = lax.broadcasted_iota(jnp.int32, (step, experts), 1)
        chosen = (ids[:, 0:1] == lanes) | (ids[:, 1:2] == lanes)
        gates_ref[rows, :] = jnp.where(chosen, probs, 0.0)
        probs_ref[rows, :] = probs


def proj(tokens, os, ws, gain, router, ids):
    length, width = tokens.shape
    experts = router.shape[1]
    sds = jax.ShapeDtypeStruct
    return pl.pallas_call(
        proj_kernel,
        out_shape=(
            sds((length, width), f32),
            sds((length, width), bf16),
            sds((length, experts), f32),
            sds((length, experts), f32),
        ),
        in_specs=[VM] * 12,
        out_specs=[VM] * 4,
        compiler_params=params(32),
        cost_estimate=cost(1_200_000_000, 14_000_000),
        name="proj",
    )(tokens, *os, *ws, gain.reshape(1, width), router, ids)


def expert_kernel(b_ref, w_ref, c_ref, gates_ref, gg_ref, du_ref, dg_ref, acc, cols):
    i = pl.program_id(0)
    per = pl.num_programs(0) // gates_ref.shape[1]
    e = i // per
    j = i % per
    length = b_ref.shape[0]
    step = 256
    k0 = 0.7978845608028654
    k1 = 0.044715

    def chunk(n, carry):
        rows = pl.ds(pl.multiple_of(n * step, step), step)
        u = dot(b_ref[rows, :], w_ref[...])
        lanes = lax.broadcasted_iota(jnp.int32, (step, gates_ref.shape[1]), 1)
        gate = jnp.sum(jnp.where(lanes == e, gates_ref[rows, :], 0.0), axis=1, keepdims=True)
        u2 = u * u
        t = jnp.tanh(u * (k0 + (k0 * k1) * u2))
        half = 0.5 + 0.5 * t
        g = u * half
        slope = half + (0.5 * u) * (1.0 - t * t) * (k0 + (3.0 * k0 * k1) * u2)
        c = c_ref[rows, :].astype(f32)
        gg_ref[rows, :] = (g * gate).astype(bf16)
        du_ref[rows, :] = (gate * c * slope).astype(bf16)
        cg = c * g
        part = cg[:, 0:128]
        for q in range(1, cg.shape[1] // 128):
            part = part + cg[:, q * 128 : (q + 1) * 128]
        total = jnp.where(j == 0, part, acc[rows, :] + part)
        acc[rows, :] = total

        @pl.when(j == per - 1)
        def _():
            lane = lax.broadcasted_iota(jnp.int32, (step, 128), 1)
            cols[rows, :] = jnp.where(
                lane == e, jnp.sum(total, axis=1, keepdims=True), cols[rows, :]
            )

        return carry

    lax.fori_loop(0, length // step, chunk, 0)

    @pl.when(i == pl.num_programs(0) - 1)
    def _():
        def turn(n, carry):
            rows = pl.ds(pl.multiple_of(n * step, step), step)
            dg_ref[:, rows] = cols[rows, :].T[:8]
            return carry

        lax.fori_loop(0, length // step, turn, 0)


def expert_pass(b, w_in, c, gates):
    length, width = b.shape
    experts, _, hidden = w_in.shape
    block = 256
    per = hidden // block
    sds = jax.ShapeDtypeStruct
    return pl.pallas_call(
        expert_kernel,
        out_shape=(
            sds((length, experts * hidden), bf16),
            sds((length, experts * hidden), bf16),
            sds((8, length), f32),
        ),
        grid_spec=pltpu.PrefetchScalarGridSpec(
            num_scalar_prefetch=0,
            grid=(experts * per,),
            in_specs=[
                pl.BlockSpec((length, width), lambda i: (0, 0)),
                pl.BlockSpec((None, width, block), lambda i: (i // per, 0, i % per)),
                pl.BlockSpec((length, block), lambda i: (0, i)),
                pl.BlockSpec((length, experts), lambda i: (0, 0)),
            ],
            out_specs=[
                pl.BlockSpec((length, block), lambda i: (0, i)),
                pl.BlockSpec((length, block), lambda i: (0, i)),
                pl.BlockSpec((8, length), lambda i: (0, 0)),
            ],
            scratch_shapes=[pltpu.VMEM((length, 128), f32), pltpu.VMEM((length, 128), f32)],
        ),
        compiler_params=params(24),
        cost_estimate=cost(10_000_000_000, 25_000_000),
        name="expert_pass",
    )(b, w_in, c, gates)


def dbuf_kernel(t_ref, du_ref, w_ref, dg_ref, keep_ref, send_ref, acc):
    e = pl.program_id(0)
    last = pl.num_programs(0) - 1
    length = du_ref.shape[0]
    count = length // 4

    def chunk(n, carry):
        rows = pl.ds(pl.multiple_of(n * count, count), count)
        got = dot(du_ref[rows, :], w_ref[...], NT)
        total = jnp.where(e == 0, got, acc[rows, :] + got)
        acc[rows, :] = total

        @pl.when(e == last)
        def _():
            r = t_ref[0] ^ n
            tail = jnp.concatenate(
                [dg_ref[:, rows], jnp.zeros((8, total.shape[1] - count), f32)], axis=1
            )

            @pl.when(r % 2 == 0)
            def _():
                keep_ref[r // 2, 0:count, :] = total
                keep_ref[r // 2, count : count + 8, :] = tail

            @pl.when(r % 2 == 1)
            def _():
                send_ref[r // 2, 0:count, :] = total
                send_ref[r // 2, count : count + 8, :] = tail

        return carry

    lax.fori_loop(0, 4, chunk, 0)


def dbuf(t, du, w_in, dg):
    length = du.shape[0]
    experts, width, hidden = w_in.shape
    sds = jax.ShapeDtypeStruct((2, length // 4 + 8, width), f32)
    whole = pl.BlockSpec((2, length // 4 + 8, width), lambda i: (0, 0, 0))
    return pl.pallas_call(
        dbuf_kernel,
        out_shape=(sds, sds),
        grid_spec=pltpu.PrefetchScalarGridSpec(
            num_scalar_prefetch=0,
            grid=(experts,),
            in_specs=[
                SM,
                pl.BlockSpec((length, hidden), lambda i: (0, i)),
                pl.BlockSpec((None, width, hidden), lambda i: (i, 0, 0)),
                pl.BlockSpec((8, length), lambda i: (0, 0)),
            ],
            out_specs=[whole, whole],
            scratch_shapes=[pltpu.VMEM((length, width), f32)],
        ),
        compiler_params=params(28),
        cost_estimate=cost(4_800_000_000, 18_000_000),
        name="dbuf",
    )(t, du, w_in, dg)


def moe_kernel(t_ref, gg_ref, w_ref, h_ref, keep_ref, send_ref, acc):
    e = pl.program_id(0)
    last = pl.num_programs(0) - 1
    length = gg_ref.shape[0]
    cols = h_ref.shape[1] // 4
    step = 256

    def chunk(n, carry):
        rows = pl.ds(pl.multiple_of(n * step, step), step)
        got = dot(gg_ref[rows, :], w_ref[...])
        acc[rows, :] = jnp.where(e == 0, got, acc[rows, :] + got)
        return carry

    lax.fori_loop(0, length // step, chunk, 0)

    @pl.when(e == last)
    def _():
        t = t_ref[0]
        for k in range(4):
            r = t ^ k
            part = slice(k * cols, (k + 1) * cols)
            for side in range(2):
                rows = slice(side * (length // 2), (side + 1) * (length // 2))
                lanes = slice(side * cols, (side + 1) * cols)

                @pl.when(r == 0)
                def _():
                    keep_ref[0, :, lanes] = acc[rows, part] + h_ref[rows, part]

                @pl.when(r == 2)
                def _():
                    keep_ref[1, :, lanes] = acc[rows, part]

                @pl.when(r % 2 == 1)
                def _():
                    send_ref[r // 2, :, lanes] = acc[rows, part]


def moe(t, gg, w_out, h):
    length, width = h.shape
    experts, hidden, _ = w_out.shape
    shape = (2, length // 2, width // 2)
    sds = jax.ShapeDtypeStruct(shape, f32)
    whole = pl.BlockSpec(shape, lambda i: (0, 0, 0))
    return pl.pallas_call(
        moe_kernel,
        out_shape=(sds, sds),
        grid_spec=pltpu.PrefetchScalarGridSpec(
            num_scalar_prefetch=0,
            grid=(experts,),
            in_specs=[
                SM,
                pl.BlockSpec((length, hidden), lambda i: (0, i)),
                pl.BlockSpec((None, hidden, width), lambda i: (i, 0, 0)),
                pl.BlockSpec((length, width), lambda i: (0, 0)),
            ],
            out_specs=[whole, whole],
            scratch_shapes=[pltpu.VMEM((length, width), f32)],
        ),
        compiler_params=params(32),
        cost_estimate=cost(4_800_000_000, 18_000_000),
        name="moe",
    )(t, gg, w_out, h)


def norm2_kernel(
    t_ref, k0_ref, r0_ref, x0_ref, h_ref, b_ref, gates_ref, probs_ref, c_ref, gain_ref, rt_ref,
    dh_ref, small_ref,
):
    count, width = dh_ref.shape
    experts = probs_ref.shape[1]
    ext = k0_ref[...] + r0_ref[...] + x0_ref[...]
    db = ext[:count]
    dgt = ext[count : count + 8, :count]
    dg = jnp.concatenate([dgt, jnp.zeros((120, count), f32)], 0).T[:, :experts]
    probs = probs_ref[...]
    dprobs = jnp.where(gates_ref[...] > 0.0, dg, 0.0)
    dlogit = probs * (dprobs - jnp.sum(probs * dprobs, axis=1, keepdims=True))
    b = b_ref[...].astype(f32)
    rows = []
    for e in range(experts):
        col = dlogit[:, e : e + 1]
        db = db + col * rt_ref[e : e + 1, :].astype(f32)
        rows.append(jnp.sum(b * col, axis=0, keepdims=True))
    h = h_ref[...]
    r = lax.rsqrt(jnp.mean(h * h, axis=1, keepdims=True) + EPS)
    rows.append(jnp.sum(db * h * r, axis=0, keepdims=True))
    rows.append(jnp.zeros((8 - experts - 1, width), f32))
    small_ref[...] = jnp.concatenate(rows, axis=0)
    weighted = db * gain_ref[...]
    inner = jnp.mean(weighted * h, axis=1, keepdims=True)
    dh_ref[...] = c_ref[...].astype(f32) + r * weighted - h * (r * r * r) * inner


def norm2_back(t, keep, got, across, h, b, gates, probs, cotangent, gain, router):
    length, width = h.shape
    count = length // 4
    experts = router.shape[1]
    first = pl.BlockSpec((None, count + 8, width), lambda i, t: (0, 0, 0))
    sds = jax.ShapeDtypeStruct

    def mine(cols):
        return pl.BlockSpec((count, cols), lambda i, t: (t[0], 0))

    return pl.pallas_call(
        norm2_kernel,
        out_shape=(sds((count, width), f32), sds((8, width), f32)),
        grid_spec=pltpu.PrefetchScalarGridSpec(
            num_scalar_prefetch=1,
            grid=(1,),
            in_specs=[
                first,
                first,
                pl.BlockSpec((count + 8, width), lambda i, t: (0, 0)),
                mine(width),
                mine(width),
                mine(experts),
                mine(experts),
                mine(width),
                pl.BlockSpec((1, width), lambda i, t: (0, 0)),
                pl.BlockSpec((experts, width), lambda i, t: (0, 0)),
            ],
            out_specs=[
                pl.BlockSpec((count, width), lambda i, t: (0, 0)),
                pl.BlockSpec((8, width), lambda i, t: (0, 0)),
            ],
        ),
        compiler_params=params(24),
        cost_estimate=cost(10_000_000, 5_000_000),
        name="norm2_back",
    )(t, keep, got, across, h, b, gates, probs, cotangent, gain.reshape(1, width), router.T)


def da_kernel(t_ref, w_ref, g_ref, xt_ref, gain_ref, r1_ref, keep_ref, send_ref, dots_ref, dgain_ref):
    count = keep_ref.shape[1]
    length = keep_ref.shape[2]
    dots = jnp.zeros((1, length), f32)
    r1 = r1_ref[...]
    for k in range(4):
        rows = slice(k * count, (k + 1) * count)
        part = dot(w_ref[0, rows, :], g_ref[0])
        for c in range(1, 3):
            part = part + dot(w_ref[c, rows, :], g_ref[c])
        dx = part * xt_ref[rows, :].astype(f32)
        dots = dots + jnp.sum(dx * gain_ref[rows, :], axis=0, keepdims=True)
        dgain_ref[rows, :] = jnp.sum(dx * r1, axis=1, keepdims=True)
        r = t_ref[0] ^ k

        @pl.when(r % 2 == 0)
        def _():
            keep_ref[r // 2] = part

        @pl.when(r % 2 == 1)
        def _():
            send_ref[r // 2] = part

    dots_ref[...] = dots


def da_pass(t, w, g, xt, gain, r1):
    width, length = xt.shape
    sds = jax.ShapeDtypeStruct
    shape = sds((2, width // 4, length), f32)
    return pl.pallas_call(
        da_kernel,
        out_shape=(shape, shape, sds((1, length), f32), sds((width, 1), f32)),
        in_specs=[SM] + [VM] * 5,
        out_specs=[VM] * 4,
        compiler_params=params(32),
        cost_estimate=cost(900_000_000, 6_000_000),
        name="da_pass",
    )(t, w, g, xt, gain.reshape(width, 1), r1)


def last_kernel(
    t_ref, k0_ref, r0_ref, x0_ref, xt_ref, gain_ref, r1_ref, dots_ref, d0, d1, d2, d3, out_ref
):
    cols = out_ref.shape[1]
    count, width = d0.shape
    t = t_ref[0]
    r1 = r1_ref[...]
    da = k0_ref[...] + r0_ref[...] + x0_ref[...]
    rows = pl.ds(pl.multiple_of(t * cols, cols), cols)
    x = xt_ref[rows, :].astype(f32)
    norm = r1 * (da * gain_ref[rows, :]) - x * (r1 * r1 * r1) * (dots_ref[...] * (1.0 / width))
    turned = norm.T
    out_ref[...] = turned
    for k in range(4):

        @pl.when(t == k)
        def _():
            for r, d in enumerate((d0, d1, d2, d3)):
                at = (k ^ r) * count
                out_ref[at : at + count, :] += d[:, k * cols : (k + 1) * cols]


def last_pass(t, keep, got, across, xt, gain, r1, dots, shards):
    width, length = xt.shape
    sds = jax.ShapeDtypeStruct
    return pl.pallas_call(
        last_kernel,
        out_shape=sds((length, width // 4), f32),
        in_specs=[SM] + [VM] * 11,
        out_specs=VM,
        compiler_params=params(32),
        cost_estimate=cost(10_000_000, 6_000_000),
        name="last_pass",
    )(t, keep[0], got[0], across, xt, gain.reshape(width, 1), r1, dots, *shards)


def ring_order(n):
    return list(range(0, n, 2)) + list(range(n - 1, 0, -2))


def ring_sums(parts, n):
    order = ring_order(n)
    place = jnp.asarray([order.index(i) for i in range(n)], jnp.int32)[lax.axis_index("dp")]
    table = jnp.asarray(order, jnp.int32)

    def piece(array, direction, step):
        rows = array.shape[0] // n
        at = table[(place - direction * (1 + step)) % n]
        return lax.dynamic_slice_in_dim(array, at * rows, rows, 0)

    moves = {
        1: [(order[i], order[(i + 1) % n]) for i in range(n)],
        -1: [(order[i], order[(i - 1) % n]) for i in range(n)],
    }
    held = [piece(a, d, 0) for a, d in parts]
    for step in range(1, n):
        came = [lax.ppermute(x, "dp", moves[d]) for x, (_, d) in zip(held, parts)]
        held = [x + piece(a, d, step) for x, (a, d) in zip(came, parts)]
    return held


def sum_over_dp(parts, n):
    rows = parts[0][0].shape[0] // n
    if n % 2 == 0 and n <= 16 and rows % 8 == 0:
        return ring_sums(parts, n)
    return [lax.psum_scatter(a, "dp", scatter_dimension=0, tiled=True) for a, _ in parts]


def on_device(
    dp_count, tokens, cotangent, gain_attn, prefix_len, bucket_ids, pos_bias, w_qkv, w_attn_out,
    gain_ffn, w_router, expert_ids, w_expert_in, w_expert_out,
):
    length, width = tokens.shape
    heads = pos_bias.shape[1]
    flat = w_attn_out.shape[0]
    experts, _, hidden = w_expert_in.shape
    t = lax.axis_index("tensor").astype(jnp.int32).reshape(1)

    def core(x):
        return lax.ppermute(x, "tensor", CORE)

    def across(x):
        return lax.ppermute(x, "tensor", ACROSS)

    wo = w_attn_out.astype(f32)
    wo_x = across(wo)
    wos = (w_attn_out, core(wo), wo_x, core(wo_x))
    ids_rev = jnp.concatenate([bucket_ids[::-1], bucket_ids[:1]])[None, :]

    a, q, kt, v, os, o = attn_fwd(prefix_len, tokens, gain_attn, w_qkv, ids_rev, pos_bias)
    o_x = across(o)
    o_shards = (o, core(o), o_x, core(o_x))
    c_w = jnp.einsum("ld,efd->lef", cotangent, w_expert_out, preferred_element_type=f32)
    c_w = c_w.astype(bf16).reshape(length, experts * hidden)
    h, b, gates, probs = proj(tokens, o_shards, wos, gain_ffn, w_router, expert_ids)
    gg, du, dg = expert_pass(b, w_expert_in, c_w, gates)

    grad_out_t = dot(cotangent, gg, TN)
    grad_in = dot(b, du, TN)
    mid = (experts // 2) * hidden

    db_keep, db_send = dbuf(t, du, w_expert_in, dg)
    db_got = core(db_send)
    db_across = across(db_keep[1] + db_got[1])
    dh, small_ffn = norm2_back(
        t, db_keep, db_got, db_across, h, b, gates, probs, cotangent, gain_ffn, w_router
    )
    dh_x = across(dh)
    dh_shards = (dh, core(dh), dh_x, core(dh_x))

    y_keep, y_send = moe(t, gg, w_expert_out, h)
    y_got = core(y_send)
    y_across = across(y_keep[1] + y_got[1])
    packed = y_keep[0] + y_got[0] + y_across
    cols = width // 4
    output = jnp.concatenate([packed[:, :cols], packed[:, cols:]], axis=0).astype(bf16)

    g, dpb = attn_bwd(
        prefix_len, t, dh_shards, w_attn_out, q, kt, v, os, ids_rev, pos_bias
    )
    g = g.reshape(3, flat, length)
    xt = tokens.T
    xf = tokens.astype(f32)
    r1 = lax.rsqrt(jnp.mean(xf * xf, axis=1) + EPS)[None, :]
    da_keep, da_send, dots, dgain = da_pass(t, w_qkv, g, xt, gain_attn, r1)

    pad = jnp.zeros((8, length - width), f32)
    small = jnp.concatenate([small_ffn, pad], axis=1)
    small = jnp.concatenate(
        [small[: experts + 1], dots, jnp.pad(dgain.T, ((0, 0), (0, length - width))), small[-1:]], axis=0
    )
    small = small + core(small)
    small = small + across(small)
    dots = small[experts + 1 : experts + 2]

    da_got = core(da_send)
    da_across = across(da_keep[1] + da_got[1])
    d_tokens = last_pass(t, da_keep, da_got, da_across, xt, gain_attn, r1, dots, dh_shards)

    d_all = jnp.zeros((length, width), bf16)
    count = length // 4
    for r, d in enumerate(dh_shards):
        d_all = lax.dynamic_update_slice_in_dim(d_all, d.astype(bf16), (t[0] ^ r) * count, 0)
    o_flat = jnp.concatenate([o[:, :flat], o[:, flat:]], axis=0).astype(bf16)
    grad_wo_t = dot(d_all, o_flat, TN)
    grad_qkv = jnp.einsum("ld,cfl->dcf", a, g, preferred_element_type=f32).reshape(width, 3 * flat)
    rows = width // dp_count
    columns = [small[: experts + 1, :width].T, small[experts + 2 : experts + 3, :width].T]
    if rows % 8 == 0:
        bias_flat = dpb.reshape(-1)
        reps = -(-bias_flat.shape[0] // rows)
        bias_cols = jnp.pad(bias_flat, (0, reps * rows - bias_flat.shape[0])).reshape(reps, rows).T
        columns.append(jnp.tile(bias_cols, (dp_count, 1)))
    tail = jnp.concatenate(columns, axis=1)
    tail = jnp.pad(tail, ((0, 0), (0, 128 - tail.shape[1])))

    sums = sum_over_dp(
        [
            (grad_out_t[:, :mid], 1),
            (grad_out_t[:, mid:], -1),
            (grad_in[:, :mid], 1),
            (grad_in[:, mid:], -1),
            (jnp.concatenate([grad_qkv[:, : 2 * flat], tail], axis=1), 1),
            (jnp.concatenate([grad_qkv[:, 2 * flat :], grad_wo_t], axis=1), -1),
        ],
        dp_count,
    )
    g_out = jnp.concatenate(sums[0:2], axis=1).T.reshape(experts, hidden, rows)
    g_in = jnp.concatenate(sums[2:4], axis=1).reshape(rows, experts, hidden).transpose(1, 0, 2)
    g_qkv = jnp.concatenate([sums[4][:, : 2 * flat], sums[5][:, :flat]], axis=1)
    g_qkv = g_qkv.reshape(rows, 3, flat).transpose(1, 0, 2)
    g_wo = sums[5][:, flat:].T
    g_small = sums[4][:, 2 * flat :]
    if rows % 8 == 0:
        bias = g_small[:, experts + 2 : experts + 2 + reps].T.reshape(-1)[: dpb.size]
        g_bias = bias.reshape(dpb.shape)
    else:
        g_bias = lax.psum(dpb, "dp")
    return (
        output, d_tokens, g_small[:, experts + 1], g_bias, g_qkv, g_wo, g_small[:, experts],
        g_small[:, :experts], g_in, g_out,
    )


def solution(mesh):
    in_specs = (
        P("dp", None), P("dp", None), P(), P("dp"), P(), P(None, "tensor"), P(None, None, "tensor"),
        P("tensor", None), P(), P(), P("dp", None), P(None, None, "tensor"), P(None, "tensor", None),
    )
    out_specs = (
        P("dp", "tensor"), P("dp", "tensor"), P("dp"), P(None, "tensor"), P(None, "dp", "tensor"),
        P("tensor", "dp"), P("dp"), P("dp", None), P(None, "dp", "tensor"), P(None, "tensor", "dp"),
    )

    def body(*args):
        return on_device(mesh.shape["dp"], *args)

    return jax.shard_map(body, mesh=mesh, in_specs=in_specs, out_specs=out_specs, check_vma=False)
```

time: 1230 us -> 456 us (0.37)
  waiting for transfers between devices: 461 us -> 126 us
  local copies, waits for them, and re-layouts: 400 us -> 78.2 us
  matrix products: 138 us -> 29.6 us
  Pallas kernels: 0 us -> 79.9 us
  blocking collectives: 62.8 us -> 0 us
  starting transfers between devices: 0.58 us -> 62.3 us
  other arithmetic: 107 us -> 47.8 us
  loops' own time: 42.1 us -> 0 us
    reduce_scatter x2 -> x0, waiting for transfers between devices: 324 us -> none  [the longest x1 165 us: on_device(): lax.psum_scatter(grad_w_out, 'dp', scatter_dimension=2, tiled=True)]
    while x90 -> x0, local copies, waits for them, and re-layouts: 162 us -> none
    ppermute x0 -> x59, waiting for transfers between devices: none -> 126 us  [the longest x42 95.3 us: ring_sums(): came = [lax.ppermute(x, 'dp', moves[d]) for x, (_, d) in zip(held, parts)]]
    dot_general x28 -> x5, matrix products: 130 us -> 29.6 us  [the longest x3 19.5 us: dot(): return lax.dot_general(a, b, dims, preferred_element_type=f32)]
    reshape x9 -> x5, local copies, waits for them, and re-layouts: 95.1 us -> 11.3 us  [the longest x1 8.88 us: on_device(): c_w = c_w.astype(bf16).reshape(length, experts * hidden)]
    pallas_call x0 -> x9, Pallas kernels: none -> 79.9 us  [the longest x1 25.4 us: expert_pass(): pl.pallas_call(expert_kernel, out_shape=(sds((length, experts * hidden),...]
    psum x3 -> x0, waiting for transfers between devices: 71.8 us -> none  [the longest x1 49.7 us: on_device(): attn_branch = lax.psum(attn_part, 'tensor')]
    unnamed x13 -> x0, waiting for transfers between devices: 65.3 us -> none
  transfers between devices with their start and end apart: 9 -> 59, of which waited for: 6 -> 31; matrix products, arithmetic and copies ran while one was open for 31% -> 25% of each run, Pallas kernels for 0% -> 6%
where the time goes in v1:
time: 456 us; the launch traced here: 448 us
  waiting for transfers between devices  126 us (28%)
  Pallas kernels  79.9 us (18%)
  local copies, waits for them, and re-layouts  78.2 us (17%)
  starting transfers between devices  62.3 us (14%)
  other arithmetic  47.8 us (10%)
  matrix products  29.6 us (6%)
  between operations  23.8 us (5%)
    ppermute x42, waiting for transfers between devices, ring_sums(): came = [lax.ppermute(x, 'dp', moves[d]) for x, (_, d) in zip(held, parts)]  95.3 us
    ppermute x42, starting transfers between devices, ring_sums(): came = [lax.ppermute(x, 'dp', moves[d]) for x, (_, d) in zip(held, parts)]  50.7 us
    unnamed x171, local copies, waits for them, and re-layouts  42.8 us
    add x42, other arithmetic, ring_sums(): held = [x + piece(a, d, step) for x, (a, d) in zip(came, parts)]  34.6 us
    ppermute x7, waiting for transfers between devices, across(): return lax.ppermute(x, 'tensor', ACROSS)  30.3 us
    pallas_call x1, Pallas kernels, expert_pass(): pl.pallas_call(expert_kernel, out_shape=(sds((length, experts * hidden),...  25.4 us
    dot_general x3, matrix products, dot(): return lax.dot_general(a, b, dims, preferred_element_type=f32)  19.5 us
    pallas_call x1, Pallas kernels, attn_fwd(): pl.pallas_call(attn_fwd_kernel, out_shape=(sds((length, width), bf16), sd...  12.4 us
  transfers between devices with their start and end apart: 59, of which 31 were waited for; matrix products, arithmetic and copies ran while one was open for 25% of the time, Pallas kernels for 6%

profile of v1, /device:TPU:0, one launch (start us, length us, event | category | flops | bytes accessed | tf_op | source)
XLA Modules:
  0.0 447.8 jit_solution(10412005780652775483)
XLA Ops:
  5.2 12.4 %attn_fwd.1 = (bf16[1024,768]{1,0:T(8,128)(2,1)S(1)}, bf16[3,1024,64]{2,1,0:T(8,128)(2,1)S(1)}, bf16[3,64,1024]{2,1,0:T(8,128)(2,1)S(1)}, bf16[3,1024,64]{2,1,0:...) custom-call(s32[1]{0:T(128)S(6)} %copy.64.prefix_ref, bf16[1024,768]{1,0:T(8,128)(2,1)S(1)} %copy-done, ...), custom_call_target="tpu_custom_call" | custom-call | flops 12000000000 | bytes 8000000 | tf_op jit(solution)/shard_map/attn_fwd/pallas_call | solution.py:109
  22.7 16.7 %collective-permute-done.1.o2 = f32[512,384]{1,0:T(8,128)} collective-permute-done((f32[512,384]{1,0:T(8,128)}, f32[512,384]{1,0:T(8,128)}, u32[]{:S(2)}, u32[]{:S(2)}) %collective-permute-start.1) | collective-permute-done | bytes 786464 | tf_op jit(solution)/shard_map/ppermute | solution.py:681
  39.4 7.1 %convolution_convert_fusion = bf16[1024,4,768]{0,2,1:T(8,128)(2,1)} fusion(bf16[4,768,768]{2,1,0:T(8,128)(2,1)S(1)} %copy-done.43, bf16[1024,768]{1,0:T(8,128)(2,1)S(1)} %copy-done.21), kind=kOutput, calls=%fused_computation.9 | convolution fusion | flops 4834983936 | bytes 12582912 | tf_op jit(solution)/shard_map/ld,efd->lef/dot_general | solution.py:691
  75.5 8.9 %copy.55.c_ref = bf16[1024,3072]{1,0:T(8,128)(2,1)} copy(bf16[1024,3072]{0,1:T(8,128)(2,1)} %bitcast.102) | data formatting | bytes 12582912 | tf_op jit(solution)/shard_map/reshape | solution.py:692
  86.9 6.4 %proj.1 = (f32[1024,768]{1,0:T(8,128)S(1)}, bf16[1024,768]{1,0:T(8,128)(2,1)S(1)}, f32[1024,4]{1,0:T(8,128)S(1)}, f32[1024,4]{1,0:T(8,128)S(1)}) custom-call(bf16[1024,768]{1,0:T(8,128)(2,1)S(1)} %copy-done, f32[512,384]{1,0:T(8,128)} %get-tuple-element.35.o0, f32[512,384]{1,0:T(8,128)} %collective-permute-done.o1, f32[512,384]{1,0:T(8,128)} %collective-permute-done.1.o2, ...), custom_call_target="tpu_custom_call" | custom-call | flops 1200000000 | bytes 14000000 | tf_op jit(solution)/shard_map/proj/pallas_call | solution.py:263
  94.2 4.2 copy-done.45
  98.4 25.4 %expert_pass.1 = (bf16[1024,3072]{1,0:T(8,128)(2,1)S(1)}, bf16[1024,3072]{1,0:T(8,128)(2,1)S(1)}, f32[8,1024]{1,0:T(8,128)S(1)}) custom-call(bf16[1024,768]{1,0:T(8,128)(2,1)S(1)} %get-tuple-element.36.b_ref, bf16[4,768,768]{2,1,0:T(8,128)(2,1)S(1)} %copy-done.45, bf16[1024,3072]{1,0:T(8,128)(2,1)S(1)} %copy-done.1, f32[1024,4]{1,0:T(8,128)S(1)} %get-tuple-element.37.gates_ref), custom_call_target="tpu_custom_call" | custom-call | flops 10000000000 | bytes 25000000 | tf_op jit(solution)/shard_map/expert_pass/pallas_call | solution.py:336
  123.9 8.0 %convolution_bitcast_fusion = f32[768,3072]{1,0:T(8,128)} fusion(bf16[1024,3072]{1,0:T(8,128)(2,1)S(1)} %get-tuple-element.38.gg_ref, bf16[1024,768]{1,0:T(8,128)(2,1)S(1)} %copy-done.22), kind=kOutput, calls=%fused_computation | convolution fusion | flops 4831838208 | bytes 17301504 | tf_op jit(solution)/shard_map/dot_general | solution.py:21
  137.0 9.4 %moe.1 = (f32[2,512,384]{2,1,0:T(8,128)S(1)}, f32[2,512,384]{2,1,0:T(8,128)S(1)}) custom-call(s32[1]{0:T(128)} %bitcast.t_ref, bf16[1024,3072]{1,0:T(8,128)(2,1)S(1)} %copy-done.50, bf16[4,768,768]{2,1,0:T(8,128)(2,1)S(1)} %copy-done.44, f32[1024,768]{1,0:T(8,128)S(1)} %get-tuple-element.39.h_ref), custom_call_target="tpu_custom_call" | custom-call | flops 4800000000 | bytes 18000000 | tf_op jit(solution)/shard_map/moe/pallas_call | solution.py:469
  146.8 11.0 %fusion.49 = f32[768,3072]{1,0:T(8,128)} fusion(bf16[1024,768]{1,0:T(8,128)(2,1)S(1)} %get-tuple-element.36.b_ref, bf16[1024,3072]{1,0:T(8,128)(2,1)} %copy-done.47), kind=kOutput, calls=%fused_computation.148 | convolution fusion | flops 4831838208 | bytes 17301504 | tf_op jit(solution)/shard_map/dot_general | solution.py:21
  157.8 8.9 %dbuf.1 = (f32[2,264,768]{2,1,0:T(8,128)S(1)}, f32[2,264,768]{2,1,0:T(8,128)S(1)}) custom-call(s32[1]{0:T(128)} %bitcast.t_ref, bf16[1024,3072]{1,0:T(8,128)(2,1)S(1)} %copy-done.48, bf16[4,768,768]{2,1,0:T(8,128)(2,1)S(1)} %bitcast.101, f32[8,1024]{1,0:T(8,128)S(1)} %get-tuple-element.43.dg_ref), custom_call_target="tpu_custom_call" | custom-call | flops 4800000000 | bytes 18000000 | tf_op jit(solution)/shard_map/dbuf/pallas_call | solution.py:404
  166.9 7.2 %fusion.44 = (f32[768,1536]{1,0:T(8,128)S(1)}, f32[768,1536]{1,0:T(8,128)}) fusion(f32[768,3072]{1,0:T(8,128)} %convolution_bitcast_fusion), kind=kLoop, calls=%fused_computation.143 | loop fusion | bytes 18874368 | tf_op jit(solution)/shard_map/slice | solution.py:757
  178.4 6.9 %fusion.45 = (f32[768,1536]{1,0:T(8,128)S(1)}, f32[768,1536]{1,0:T(8,128)}) fusion(f32[768,3072]{1,0:T(8,128)} %fusion.49), kind=kLoop, calls=%fused_computation.144 | loop fusion | bytes 18874368 | tf_op jit(solution)/shard_map/slice | solution.py:759
  198.3 6.3 %collective-permute-done.38 = f32[96,1536]{1,0:T(8,128)S(1)} collective-permute-done((f32[96,1536]{1,0:T(8,128)S(1)}, f32[96,1536]{1,0:T(8,128)S(1)}, u32[]{:S(2)}, u32[]{:S(2)}) %collective-permute-start.38) | collective-permute-done | bytes 589856 | tf_op jit(solution)/shard_map/ppermute | solution.py:655
  209.4 7.9 %collective-permute-done.53 = f32[96,1536]{1,0:T(8,128)S(1)} collective-permute-done((f32[96,1536]{1,0:T(8,128)S(1)}, f32[96,1536]{1,0:T(8,128)S(1)}, u32[]{:S(2)}, u32[]{:S(2)}) %collective-permute-start.53) | collective-permute-done | bytes 589856 | tf_op jit(solution)/shard_map/ppermute | solution.py:655
  223.1 6.9 %collective-permute-done.39 = f32[96,1536]{1,0:T(8,128)S(1)} collective-permute-done((f32[96,1536]{1,0:T(8,128)S(1)}, f32[96,1536]{1,0:T(8,128)S(1)}, u32[]{:S(2)}, u32[]{:S(2)}) %collective-permute-start.39) | collective-permute-done | bytes 589856 | tf_op jit(solution)/shard_map/ppermute | solution.py:655
  249.2 6.0 %collective-permute-done.40 = f32[96,1536]{1,0:T(8,128)S(1)} collective-permute-done((f32[96,1536]{1,0:T(8,128)S(1)}, f32[96,1536]{1,0:T(8,128)S(1)}, u32[]{:S(2)}, u32[]{:S(2)}) %collective-permute-start.40) | collective-permute-done | bytes 589856 | tf_op jit(solution)/shard_map/ppermute | solution.py:655
  259.9 7.9 %collective-permute-done.55 = f32[96,1536]{1,0:T(8,128)S(1)} collective-permute-done((f32[96,1536]{1,0:T(8,128)S(1)}, f32[96,1536]{1,0:T(8,128)S(1)}, u32[]{:S(2)}, u32[]{:S(2)}) %collective-permute-start.55) | collective-permute-done | bytes 589856 | tf_op jit(solution)/shard_map/ppermute | solution.py:655
  274.3 6.2 %collective-permute-done.41 = f32[96,1536]{1,0:T(8,128)S(1)} collective-permute-done((f32[96,1536]{1,0:T(8,128)S(1)}, f32[96,1536]{1,0:T(8,128)S(1)}, u32[]{:S(2)}, u32[]{:S(2)}) %collective-permute-start.41) | collective-permute-done | bytes 589856 | tf_op jit(solution)/shard_map/ppermute | solution.py:655
  313.0 8.8 %collective-permute-done.11.d2_ref.d2 = f32[256,768]{1,0:T(8,128)S(1)} collective-permute-done((f32[256,768]{1,0:T(8,128)S(1)}, f32[256,768]{1,0:T(8,128)S(1)}, u32[]{:S(2)}, u32[]{:S(2)}) %collective-permute-start.11) | collective-permute-done | bytes 786464 | tf_op jit(solution)/shard_map/ppermute | solution.py:681
  328.5 5.0 %collective-permute-done.43 = f32[96,1536]{1,0:T(8,128)S(1)} collective-permute-done((f32[96,1536]{1,0:T(8,128)S(1)}, f32[96,1536]{1,0:T(8,128)S(1)}, u32[]{:S(2)}, u32[]{:S(2)}) %collective-permute-start.43) | collective-permute-done | bytes 589856 | tf_op jit(solution)/shard_map/ppermute | solution.py:655
  339.5 11.9 %attn_bwd.1 = (bf16[3,3,64,1024]{3,2,1,0:T(8,128)(2,1)S(1)}, f32[32,3]{1,0:T(8,128)S(1)}) custom-call(s32[1]{0:T(128)S(6)} %copy.64.prefix_ref, s32[1]{0:T(128)} %bitcast.t_ref, f32[256,768]{1,0:T(8,128)S(1)} %get-tuple-element.47.d0_ref.d0, f32[256,768]{1,0:T(8,128)S(1)} %collective-permute-done.10.d1_ref.d1, ...), custom_call_target="tpu_custom_call" | custom-call | flops 12000000000 | bytes 8000000 | tf_op jit(solution)/shard_map/attn_bwd/pallas_call | solution.py:214
  409.4 4.4 collective-permute-done.21
  414.2 8.6 %collective-permute-done.22 = f32[96,512]{0,1:T(8,128)S(1)} collective-permute-done((f32[96,512]{0,1:T(8,128)S(1)}, f32[96,512]{0,1:T(8,128)S(1)}, u32[]{:S(2)}, u32[]{:S(2)}) %collective-permute-start.22) | collective-permute-done | bytes 196640 | tf_op jit(solution)/shard_map/ppermute | solution.py:655
  (379 shorter events, 211.8 us)
Async XLA Ops:
  20.7 65.7 %collective-permute-start = (f32[512,384]{1,0:T(8,128)}, f32[512,384]{1,0:T(8,128)}, u32[]{:S(2)}, u32[]{:S(2)}) collective-permute-start(f32[512,384]{1,0:T(8,128)} %get-tuple-element.35.o0), channel_id=1, source_target_pairs={{0,1},{1,0},{2,3},{3,2},{4,5},{5,4},{6,7},{7,6},{8,9},{9,8},{10,11... | collective-permute-start | bytes 2359304 | tf_op jit(solution)/shard_map/ppermute | solution.py:678
  21.5 64.9 %collective-permute-start.3 = (f32[192,768]{1,0:T(8,128)}, f32[192,768]{1,0:T(8,128)}, u32[]{:S(2)}, u32[]{:S(2)}) collective-permute-start(f32[192,768]{1,0:T(8,128)} %convert_element_type.27), channel_id=1, source_target_pairs={{0,1},{1,0},{2,3},{3,2},{4,5},{5,4},{6,7},{7,6},{8,9},{9,8},{10,11... | collective-permute-start | bytes 1769480 | tf_op jit(solution)/shard_map/ppermute | solution.py:678
  22.0 62.5 %collective-permute-start.4 = (f32[192,768]{1,0:T(8,128)}, f32[192,768]{1,0:T(8,128)}, u32[]{:S(2)}, u32[]{:S(2)}) collective-permute-start(f32[192,768]{1,0:T(8,128)} %convert_element_type.27), channel_id=1, source_target_pairs={{0,2},{2,0},{1,3},{3,1},{4,6},{6,4},{5,7},{7,5},{8,10},{10,8},{9,1... | collective-permute-start | bytes 1769480 | tf_op jit(solution)/shard_map/ppermute | solution.py:681
  39.4 47.6 %collective-permute-start.2 = (f32[512,384]{1,0:T(8,128)}, f32[512,384]{1,0:T(8,128)}, u32[]{:S(2)}, u32[]{:S(2)}) collective-permute-start(f32[512,384]{1,0:T(8,128)} %collective-permute-done.1.o2), channel_id=1, source_target_pairs={{0,1},{1,0},{2,3},{3,2},{4,5},{5,4},{6,7},{7,6},{8,9},{9,8},{10,11... | collective-permute-start | bytes 2359304 | tf_op jit(solution)/shard_map/ppermute | solution.py:678
  146.3 88.3 %collective-permute-start.6 = (f32[2,512,384]{2,1,0:T(8,128)S(1)}, f32[2,512,384]{2,1,0:T(8,128)}, u32[]{:S(2)}, u32[]{:S(2)}) collective-permute-start(f32[2,512,384]{2,1,0:T(8,128)S(1)} %get-tuple-element.41), channel_id=1, source_target_pairs={{0,1},{1,0},{2,3},{3,2},{4,5},{5,4},{6,7},{7,6},{8,9},{9,8},{10,11... | collective-permute-start | bytes 4718600 | tf_op jit(solution)/shard_map/ppermute | solution.py:678
  166.7 69.8 %collective-permute-start.8 = (f32[2,264,768]{2,1,0:T(8,128)S(1)}, f32[2,264,768]{2,1,0:T(8,128)S(1)}, u32[]{:S(2)}, u32[]{:S(2)}) collective-permute-start(f32[2,264,768]{2,1,0:T(8,128)S(1)} %get-tuple-element.45), channel_id=1, source_target_pairs={{0,1},{1,0},{2,3},{3,2},{4,5},{5,4},{6,7},{7,6},{8,9},{9,8},{10,11... | collective-permute-start | bytes 4866056 | tf_op jit(solution)/shard_map/ppermute | solution.py:678
  207.9 22.0 %collective-permute-start.39 = (f32[96,1536]{1,0:T(8,128)S(1)}, f32[96,1536]{1,0:T(8,128)S(1)}, u32[]{:S(2)}, u32[]{:S(2)}) collective-permute-start(f32[96,1536]{1,0:T(8,128)S(1)} %dynamic-slice_add_fusion.20), channel_id=1, source_target_pairs={{0,4},{8,0},{16,8},{24,16},{28,24},{20,28},{12,20},{4,12},{1,5},{9... | collective-permute-start | bytes 1769480 | tf_op jit(solution)/shard_map/ppermute | solution.py:655
  220.5 22.0 %collective-permute-start.54 = (f32[96,1536]{1,0:T(8,128)S(1)}, f32[96,1536]{1,0:T(8,128)S(1)}, u32[]{:S(2)}, u32[]{:S(2)}) collective-permute-start(f32[96,1536]{1,0:T(8,128)S(1)} %dynamic-slice_add_fusion.5), channel_id=1, source_target_pairs={{0,4},{8,0},{16,8},{24,16},{28,24},{20,28},{12,20},{4,12},{1,5},{9... | collective-permute-start | bytes 1769480 | tf_op jit(solution)/shard_map/ppermute | solution.py:655
  233.2 22.0 %collective-permute-start.40 = (f32[96,1536]{1,0:T(8,128)S(1)}, f32[96,1536]{1,0:T(8,128)S(1)}, u32[]{:S(2)}, u32[]{:S(2)}) collective-permute-start(f32[96,1536]{1,0:T(8,128)S(1)} %dynamic-slice_add_fusion.19), channel_id=1, source_target_pairs={{0,4},{8,0},{16,8},{24,16},{28,24},{20,28},{12,20},{4,12},{1,5},{9... | collective-permute-start | bytes 1769480 | tf_op jit(solution)/shard_map/ppermute | solution.py:655
  234.7 23.8 %collective-permute-start.33 = (f32[96,1536]{1,0:T(8,128)S(1)}, f32[96,1536]{1,0:T(8,128)S(1)}, u32[]{:S(2)}, u32[]{:S(2)}) collective-permute-start(f32[96,1536]{1,0:T(8,128)S(1)} %dynamic-slice_add_fusion.26), channel_id=1, source_target_pairs={{0,8},{8,16},{16,24},{24,28},{28,20},{20,12},{12,4},{4,0},{1,9},{9... | collective-permute-start | bytes 1769480 | tf_op jit(solution)/shard_map/ppermute | solution.py:655
  236.6 49.2 %collective-permute-start.7 = (f32[512,384]{1,0:T(8,128)S(1)}, f32[512,384]{1,0:T(8,128)S(1)}, u32[]{:S(2)}, u32[]{:S(2)}) collective-permute-start(f32[512,384]{1,0:T(8,128)S(1)} %fusion.3), channel_id=1, source_target_pairs={{0,2},{2,0},{1,3},{3,1},{4,6},{6,4},{5,7},{7,5},{8,10},{10,8},{9,1... | collective-permute-start | bytes 2359304 | tf_op jit(solution)/shard_map/ppermute | solution.py:681
  242.6 48.2 %collective-permute-start.9 = (f32[264,768]{1,0:T(8,128)}, f32[264,768]{1,0:T(8,128)}, u32[]{:S(2)}, u32[]{:S(2)}) collective-permute-start(f32[264,768]{1,0:T(8,128)} %fusion.1), channel_id=1, source_target_pairs={{0,2},{2,0},{1,3},{3,1},{4,6},{6,4},{5,7},{7,5},{8,10},{10,8},{9,1... | collective-permute-start | bytes 2433032 | tf_op jit(solution)/shard_map/ppermute | solution.py:681
  258.4 22.0 %collective-permute-start.41 = (f32[96,1536]{1,0:T(8,128)S(1)}, f32[96,1536]{1,0:T(8,128)S(1)}, u32[]{:S(2)}, u32[]{:S(2)}) collective-permute-start(f32[96,1536]{1,0:T(8,128)S(1)} %dynamic-slice_add_fusion.18), channel_id=1, source_target_pairs={{0,4},{8,0},{16,8},{24,16},{28,24},{20,28},{12,20},{4,12},{1,5},{9... | collective-permute-start | bytes 1769480 | tf_op jit(solution)/shard_map/ppermute | solution.py:655
  271.8 29.9 %collective-permute-start.56 = (f32[96,1536]{1,0:T(8,128)}, f32[96,1536]{1,0:T(8,128)}, u32[]{:S(2)}, u32[]{:S(2)}) collective-permute-start(f32[96,1536]{1,0:T(8,128)} %dynamic-slice_add_fusion.3), channel_id=1, source_target_pairs={{0,4},{8,0},{16,8},{24,16},{28,24},{20,28},{12,20},{4,12},{1,5},{9... | collective-permute-start | bytes 1769480 | tf_op jit(solution)/shard_map/ppermute | solution.py:655
  280.5 24.1 %collective-permute-start.49 = (f32[96,1536]{1,0:T(8,128)}, f32[96,1536]{1,0:T(8,128)}, u32[]{:S(2)}, u32[]{:S(2)}) collective-permute-start(f32[96,1536]{1,0:T(8,128)} %dynamic-slice_add_fusion.10), channel_id=1, source_target_pairs={{0,8},{8,16},{16,24},{24,28},{28,20},{20,12},{12,4},{4,0},{1,9},{9... | collective-permute-start | bytes 1769480 | tf_op jit(solution)/shard_map/ppermute | solution.py:655
  283.5 23.9 %collective-permute-start.42 = (f32[96,1536]{1,0:T(8,128)}, f32[96,1536]{1,0:T(8,128)}, u32[]{:S(2)}, u32[]{:S(2)}) collective-permute-start(f32[96,1536]{1,0:T(8,128)} %dynamic-slice_add_fusion.17), channel_id=1, source_target_pairs={{0,4},{8,0},{16,8},{24,16},{28,24},{20,28},{12,20},{4,12},{1,5},{9... | collective-permute-start | bytes 1769480 | tf_op jit(solution)/shard_map/ppermute | solution.py:655
  285.8 23.5 %collective-permute-start.35 = (f32[96,1536]{1,0:T(8,128)}, f32[96,1536]{1,0:T(8,128)}, u32[]{:S(2)}, u32[]{:S(2)}) collective-permute-start(f32[96,1536]{1,0:T(8,128)} %dynamic-slice_add_fusion.24), channel_id=1, source_target_pairs={{0,8},{8,16},{16,24},{24,28},{28,20},{20,12},{12,4},{4,0},{1,9},{9... | collective-permute-start | bytes 1769480 | tf_op jit(solution)/shard_map/ppermute | solution.py:655
  309.3 24.1 %collective-permute-start.43 = (f32[96,1536]{1,0:T(8,128)S(1)}, f32[96,1536]{1,0:T(8,128)S(1)}, u32[]{:S(2)}, u32[]{:S(2)}) collective-permute-start(f32[96,1536]{1,0:T(8,128)S(1)} %dynamic-slice_add_fusion.16), channel_id=1, source_target_pairs={{0,4},{8,0},{16,8},{24,16},{28,24},{20,28},{12,20},{4,12},{1,5},{9... | collective-permute-start | bytes 1769480 | tf_op jit(solution)/shard_map/ppermute | solution.py:655
  312.2 24.7 %collective-permute-start.36 = (f32[96,1536]{1,0:T(8,128)S(1)}, f32[96,1536]{1,0:T(8,128)S(1)}, u32[]{:S(2)}, u32[]{:S(2)}) collective-permute-start(f32[96,1536]{1,0:T(8,128)S(1)} %dynamic-slice_add_fusion.23), channel_id=1, source_target_pairs={{0,8},{8,16},{16,24},{24,28},{28,20},{20,12},{12,4},{4,0},{1,9},{9... | collective-permute-start | bytes 1769480 | tf_op jit(solution)/shard_map/ppermute | solution.py:655
  324.3 41.3 %collective-permute-start.58 = (f32[96,1536]{1,0:T(8,128)}, f32[96,1536]{1,0:T(8,128)}, u32[]{:S(2)}, u32[]{:S(2)}) collective-permute-start(f32[96,1536]{1,0:T(8,128)} %dynamic-slice_add_fusion.1), channel_id=1, source_target_pairs={{0,4},{8,0},{16,8},{24,16},{28,24},{20,28},{12,20},{4,12},{1,5},{9... | collective-permute-start | bytes 1769480 | tf_op jit(solution)/shard_map/ppermute | solution.py:655
  327.8 40.7 %collective-permute-start.51 = (f32[96,1536]{1,0:T(8,128)}, f32[96,1536]{1,0:T(8,128)}, u32[]{:S(2)}, u32[]{:S(2)}) collective-permute-start(f32[96,1536]{1,0:T(8,128)} %dynamic-slice_add_fusion.8), channel_id=1, source_target_pairs={{0,8},{8,16},{16,24},{24,28},{28,20},{20,12},{12,4},{4,0},{1,9},{9... | collective-permute-start | bytes 1769480 | tf_op jit(solution)/shard_map/ppermute | solution.py:655
  335.4 35.0 %collective-permute-start.44 = (f32[96,1536]{1,0:T(8,128)}, f32[96,1536]{1,0:T(8,128)}, u32[]{:S(2)}, u32[]{:S(2)}) collective-permute-start(f32[96,1536]{1,0:T(8,128)} %dynamic-slice_add_fusion.15), channel_id=1, source_target_pairs={{0,4},{8,0},{16,8},{24,16},{28,24},{20,28},{12,20},{4,12},{1,5},{9... | collective-permute-start | bytes 1769480 | tf_op jit(solution)/shard_map/ppermute | solution.py:655
  338.9 32.9 %collective-permute-start.37 = (f32[96,1536]{1,0:T(8,128)}, f32[96,1536]{1,0:T(8,128)}, u32[]{:S(2)}, u32[]{:S(2)}) collective-permute-start(f32[96,1536]{1,0:T(8,128)} %dynamic-slice_add_fusion.22), channel_id=1, source_target_pairs={{0,8},{8,16},{16,24},{24,28},{28,20},{20,12},{12,4},{4,0},{1,9},{9... | collective-permute-start | bytes 1769480 | tf_op jit(solution)/shard_map/ppermute | solution.py:655
  364.3 59.1 %collective-permute-start.13 = (f32[2,192,1024]{2,1,0:T(8,128)}, f32[2,192,1024]{2,1,0:T(8,128)S(1)}, u32[]{:S(2)}, u32[]{:S(2)}) collective-permute-start(f32[2,192,1024]{2,1,0:T(8,128)} %copy-done.46), channel_id=1, source_target_pairs={{0,1},{1,0},{2,3},{3,2},{4,5},{5,4},{6,7},{7,6},{8,9},{9,8},{10,11... | collective-permute-start | bytes 4718600 | tf_op jit(solution)/shard_map/ppermute | solution.py:678
  (115 other events, 1434.0 us)
